TPU v7x, 32 devices: a whole 2x2x4 slice. The times are simulated.
32 devices in a mesh: row: 4 (over z), col: 8 (over y, x, core).
Axes of the slice: x: 2, y: 2, z: 4, core: 2. Of those that a mesh axis runs over, the one named last changes fastest.
Arguments:
- kernel: bfloat16 [16384, 16384], P('row', 'col'), may hold values from -6 to 6
- labels: int32 [3, 16384], replicated, may hold values from 0 to 63, as said below
Outputs:
- distance: float32 [3, 16384, 64], P(None, ('row', 'col'))
- objective: float32 [3], replicated
Inputs may be any that keep to these rules, and one draw needn't show every extreme that they name: `labels`: in every iteration every cluster of 0 to 63 is named by at least one series.
All inputs are finite; a program needn't handle non-finite values.
Results may differ from a plain program's by a relative error of at most 0.0003.
Values sent between devices are 32-bit elements; how exact they have to be, the bound alone decides.
A program may use at most 64 MiB of HBM per device.

v0:
```python
import jax
import jax.numpy as jnp
from jax import lax
from jax.sharding import PartitionSpec as P

SERIES = 16384
CLUSTERS = 64
ITERS = 3


def shards(kernel, labels):
    rows_block, cols_block = kernel.shape
    slice_rows = rows_block // lax.axis_size("col")
    row_base = lax.axis_index("row") * rows_block
    col_base = lax.axis_index("col") * cols_block
    my_offset = lax.axis_index("col") * slice_rows
    clusters = jnp.arange(CLUSTERS, dtype=jnp.int32)
    col_labels = lax.dynamic_slice_in_dim(labels, col_base, cols_block, 1)
    block_labels = lax.dynamic_slice_in_dim(labels, row_base, rows_block, 1)
    counts = jnp.sum((labels[:, :, None] == clusters).astype(jnp.float32), axis=1)

    def encode(chosen):
        flat = chosen.T[:, :, None] == clusters[None, None, :]
        return flat.reshape(chosen.shape[1], -1).astype(jnp.bfloat16)

    local = jnp.dot(kernel, encode(col_labels), preferred_element_type=jnp.float32)
    whole = lax.psum(local, "col")
    totals = lax.psum(jnp.sum(encode(block_labels).astype(jnp.float32) * whole, axis=0), "row")
    sums = lax.dynamic_slice_in_dim(whole, my_offset, slice_rows, 0)
    sums, totals = (sums, totals)
    sums = sums.reshape(slice_rows, ITERS, CLUSTERS).transpose(1, 0, 2)
    totals = totals.reshape(ITERS, CLUSTERS)
    distance = -2.0 * sums / counts[:, None, :] + totals[:, None, :] / (counts * counts)[:, None, :]
    objective = 1.0 - jnp.sum(totals / counts, axis=1) / SERIES
    return (distance, objective)


def solution(mesh):
    return jax.shard_map(
        shards,
        mesh=mesh,
        in_specs=(P("row", "col"), P()),
        out_specs=(P(None, ("row", "col"), None), P()),
        check_vma=False,
    )
```

profile of v0, /device:TPU:0, one launch (start us, length us, event | category | flops | bytes accessed | tf_op | source)
XLA Modules:
  0.0 117.1 jit_solution(2459755366757021118)
XLA Ops:
  7.2 0.0 all-reduce.2.cloned.1.call-start
  7.2 0.1 eq.56
  7.3 0.8 dynamic-slice_bitcast_fusion.1
  8.1 0.3 bitcast_compare_fusion.1
  8.4 13.0 %convolution_bitcast_fusion = f32[4096,192]{0,1:T(8,128)} fusion(pred[2048,192]{0,1:T(32,128)(4,1)S(1)} %bitcast_compare_fusion.1, bf16[4096,2048]{1,0:T(8,128)(2,1)} %param.2), kind=kOutput, calls=%fused_computation.2 | convolution fusion | flops 3221225472 | bytes 20316160 | tf_op jit(solution)/shard_map/dot_general | solution.py:26
  21.4 0.0 copy-start
  21.4 0.0 all-reduce.2.cloned.1.call-update
  21.4 0.9 copy-done
  22.4 0.5 bitcast_compare_fusion
  22.9 2.0 %convert_reduce_fusion = f32[3,64]{1,0:T(4,128)S(1)} fusion(s32[3,16384]{1,0:T(4,128)S(1)} %copy-done), kind=kLoop, calls=%fused_computation | loop fusion | flops 9436992 | bytes 197376 | tf_op jit(solution)/shard_map/reduce_sum | solution.py:20
  24.9 68.7 %all-reduce.2.cloned.1.call-done = f32[4096,192]{0,1:T(8,128)} async-done(((f32[4096,192]{0,1:T(8,128)}), f32[4096,192]{0,1:T(8,128)}) %all-reduce.2.cloned.1.call-update) | async-done | bytes 3145744 | tf_op jit(solution)/shard_map/psum | solution.py:27
  93.6 2.4 %multiply_reduce_fusion = f32[192]{0:T(256)S(1)} fusion(f32[4096,192]{0,1:T(8,128)} %all-reduce.2.cloned.1.call-done, pred[4096,192]{0,1:T(8,128)(4,1)S(1)} %bitcast_compare_fusion), kind=kLoop, calls=%fused_computation.4 | loop fusion | flops 3145536 | bytes 3932928 | tf_op jit(solution)/shard_map/reduce_sum | solution.py:28
  96.0 0.1 broadcast_in_dim_reshape.3
  96.1 11.7 %psum.15 = f32[3,64]{1,0:T(4,128)S(1)} all-reduce(f32[3,64]{1,0:T(4,128)S(1)} %broadcast_in_dim_reshape.3), channel_id=1, replica_groups=mesh['row'=4,'col'=8] {'row'}, use_global_device_ids=true, to_apply=%region_3.0 | all-reduce | flops 192 | bytes 1536 | tf_op jit(solution)/shard_map/psum | solution.py:28
  107.8 0.1 divide_reduce_fusion
  107.9 0.5 multiply_subtract_fusion
  108.4 1.0 dynamic-slice_multiply_fusion
  109.4 0.9 add_bitcast_fusion
  (2 shorter events, 0.0 us)
Async XLA Ops:
  7.2 86.4 %all-reduce.2.cloned.1.call-start = ((), (), s32[]{:S(2)}) async-start(), calls=%async_computation | async-start | bytes 6291456 | tf_op jit(solution)/shard_map/psum | solution.py:27
  21.4 0.9 copy-start
Sparse Core Ops, SparseCore 0:
  21.6 71.9 all-reduce.1
where the time goes:
time: 117 us
  waiting for transfers between devices  68.8 us (59%)
  between operations  14.1 us (12%)
  matrix products  13 us (11%)
  blocking collectives  11.7 us (10%)
  other arithmetic  7.7 us (7%)
  local copies, waits for them, and re-layouts  1.86 us (2%)
    psum x1, waiting for transfers between devices, shards(): whole = lax.psum(local, 'col')  68.7 us
    dot_general x1, matrix products, shards(): jnp.dot(kernel, encode(col_labels), preferred_element_type=jnp.float32)  13 us
    psum x1, blocking collectives, shards(): lax.psum(jnp.sum(encode(block_labels).astype(jnp.float32) * whole, axis=0...  11.7 us
    reduce_sum x1, other arithmetic, shards(): jnp.sum(encode(block_labels).astype(jnp.float32) * whole, axis=0)  2.41 us
  transfers between devices with their start and end apart: 1, of which 1 were waited for; matrix products, arithmetic and copies ran while one was open for 2% of the time, Pallas kernels for 0%

commit v1 on v0

--- a/solution.py
+++ b/solution.py
@@ -24,7 +24,11 @@
         return flat.reshape(chosen.shape[1], -1).astype(jnp.bfloat16)
 
     local = jnp.dot(kernel, encode(col_labels), preferred_element_type=jnp.float32)
-    whole = lax.psum(local, "col")
+    devices = lax.axis_size("col")
+    whole, hop = (local, 1)
+    while hop < devices:
+        whole = whole + lax.ppermute(whole, "col", [(i, i ^ hop) for i in range(devices)])
+        hop = 2 * hop
     totals = lax.psum(jnp.sum(encode(block_labels).astype(jnp.float32) * whole, axis=0), "row")
     sums = lax.dynamic_slice_in_dim(whole, my_offset, slice_rows, 0)
     sums, totals = (sums, totals)

time: 117 us -> 178 us (1.52)
  waiting for transfers between devices: 68.8 us -> 138 us
  between operations: 14.1 us -> 0.68 us
  starting transfers between devices: 0.04 us -> 5.3 us
  matrix products: 13 us -> 9.14 us
  other arithmetic: 7.7 us -> 11.3 us
    ppermute x0 -> x3, waiting for transfers between devices: none -> 138 us  [shards(): lax.ppermute(whole, 'col', [(i, i ^ hop) for i in range(devices)])]
    psum x1 -> x0, waiting for transfers between devices: 68.7 us -> none  [shards(): whole = lax.psum(local, 'col')]
    ppermute x0 -> x3, starting transfers between devices: none -> 5.3 us  [shards(): lax.ppermute(whole, 'col', [(i, i ^ hop) for i in range(devices)])]
    dot_general x1, matrix products: 13 us -> 9.14 us  [shards(): jnp.dot(kernel, encode(col_labels), preferred_element_type=jnp.float32)]
    reduce_sum x1, other arithmetic: 2.41 us -> 4.43 us  [shards(): jnp.sum(encode(block_labels).astype(jnp.float32) * whole, axis=0)]
  transfers between devices with their start and end apart: 1 -> 3, of which waited for: 1 -> 3; matrix products, arithmetic and copies ran while one was open for 2% -> 2% of each run, Pallas kernels for 0% -> 0%
where the time goes in v1:
time: 178 us; the launch traced here: 177 us
  waiting for transfers between devices  138 us (78%)
  blocking collectives  11.9 us (7%)
  other arithmetic  11.3 us (6%)
  matrix products  9.14 us (5%)
  starting transfers between devices  5.3 us (3%)
    ppermute x3, waiting for transfers between devices, shards(): lax.ppermute(whole, 'col', [(i, i ^ hop) for i in range(devices)])  138 us
    psum x1, blocking collectives, shards(): lax.psum(jnp.sum(encode(block_labels).astype(jnp.float32) * whole, axis=0...  11.9 us
    dot_general x1, matrix products, shards(): jnp.dot(kernel, encode(col_labels), preferred_element_type=jnp.float32)  9.14 us
    ppermute x3, starting transfers between devices, shards(): lax.ppermute(whole, 'col', [(i, i ^ hop) for i in range(devices)])  5.3 us
    reduce_sum x1, other arithmetic, shards(): jnp.sum(encode(block_labels).astype(jnp.float32) * whole, axis=0)  4.43 us
  transfers between devices with their start and end apart: 3, of which 3 were waited for; matrix products, arithmetic and copies ran while one was open for 2% of the time, Pallas kernels for 0%

profile of v1, /device:TPU:0, one launch (start us, length us, event | category | flops | bytes accessed | tf_op | source)
XLA Modules:
  0.0 177.5 jit_solution(6028146422009010286)
XLA Ops:
  0.6 0.1 eq.56
  0.7 0.8 dynamic-slice_bitcast_fusion.1
  1.5 0.3 bitcast_compare_fusion.1
  1.8 9.1 %convolution_bitcast_fusion = f32[4096,192]{0,1:T(8,128)S(1)} fusion(pred[2048,192]{0,1:T(32,128)(4,1)S(1)} %bitcast_compare_fusion.1, bf16[4096,2048]{1,0:T(8,128)(2,1)} %param.2), kind=kOutput, calls=%fused_computation.2 | convolution fusion | flops 3221225472 | bytes 20316160 | tf_op jit(solution)/shard_map/dot_general | solution.py:26
  10.9 0.6 collective-permute-start
  11.5 5.3 %collective-permute-done = f32[4096,192]{0,1:T(8,128)S(1)} collective-permute-done((f32[4096,192]{0,1:T(8,128)S(1)}, f32[4096,192]{0,1:T(8,128)S(1)}, u32[]{:S(2)}, u32[]{:S(2)}) %collective-permute-start) | collective-permute-done | bytes 3145760 | tf_op jit(solution)/shard_map/ppermute | solution.py:30
  16.8 0.3 add.32
  17.1 0.0 copy-start
  17.1 2.9 %collective-permute-start.1 = (f32[4096,192]{0,1:T(8,128)S(1)}, f32[4096,192]{0,1:T(8,128)S(1)}, u32[]{:S(2)}, u32[]{:S(2)}) collective-permute-start(f32[4096,192]{0,1:T(8,128)S(1)} %add.32), channel_id=1, source_target_pairs={{0,2},{1,3},{2,0},{3,1},{4,6},{5,7},{6,4},{7,5},{8,10},{9,11},{10,... | collective-permute-start | bytes 9437192 | tf_op jit(solution)/shard_map/ppermute | solution.py:30
  20.0 68.4 %collective-permute-done.1 = f32[4096,192]{0,1:T(8,128)S(1)} collective-permute-done((f32[4096,192]{0,1:T(8,128)S(1)}, f32[4096,192]{0,1:T(8,128)S(1)}, u32[]{:S(2)}, u32[]{:S(2)}) %collective-permute-start.1) | collective-permute-done | bytes 3145760 | tf_op jit(solution)/shard_map/ppermute | solution.py:30
  88.4 0.3 add.33
  88.8 1.8 %collective-permute-start.2 = (f32[4096,192]{0,1:T(8,128)S(1)}, f32[4096,192]{0,1:T(8,128)}, u32[]{:S(2)}, u32[]{:S(2)}) collective-permute-start(f32[4096,192]{0,1:T(8,128)S(1)} %add.33), channel_id=1, source_target_pairs={{0,4},{1,5},{2,6},{3,7},{4,0},{5,1},{6,2},{7,3},{8,12},{9,13},{10,... | collective-permute-start | bytes 9437192 | tf_op jit(solution)/shard_map/ppermute | solution.py:30
  90.6 0.0 copy-done
  90.6 1.4 bitcast_compare_fusion
  92.0 2.0 %convert_reduce_fusion = f32[3,64]{1,0:T(4,128)S(1)} fusion(s32[3,16384]{1,0:T(4,128)S(1)} %copy-done), kind=kLoop, calls=%fused_computation | loop fusion | flops 9436992 | bytes 197376 | tf_op jit(solution)/shard_map/reduce_sum | solution.py:20
  94.0 64.5 %collective-permute-done.2 = f32[4096,192]{0,1:T(8,128)} collective-permute-done((f32[4096,192]{0,1:T(8,128)S(1)}, f32[4096,192]{0,1:T(8,128)}, u32[]{:S(2)}, u32[]{:S(2)}) %collective-permute-start.2) | collective-permute-done | bytes 3145760 | tf_op jit(solution)/shard_map/ppermute | solution.py:30
  158.5 4.4 %multiply_reduce_fusion = (f32[192]{0:T(256)S(1)}, f32[4096,192]{0,1:T(8,128)}) fusion(pred[4096,192]{0,1:T(8,128)(4,1)} %bitcast_compare_fusion, f32[4096,192]{0,1:T(8,128)S(1)} %add.33, f32[4096,192]{0,1:T(8,128)} %collective-permute-done.2), kind=kLoop, calls=%fused_computation.4 | loop fusion | flops 3931968 | bytes 10224384 | tf_op jit(solution)/shard_map/reduce_sum | solution.py:32
  162.9 0.1 broadcast_in_dim_reshape.3
  163.0 11.9 %psum.7 = f32[3,64]{1,0:T(4,128)S(1)} all-reduce(f32[3,64]{1,0:T(4,128)S(1)} %broadcast_in_dim_reshape.3), channel_id=1, replica_groups=mesh['row'=4,'col'=8] {'row'}, use_global_device_ids=true, to_apply=%region_2.0 | all-reduce | flops 192 | bytes 1536 | tf_op jit(solution)/shard_map/psum | solution.py:32
  174.9 0.1 divide_reduce_fusion
  175.1 0.5 multiply_subtract_fusion
  175.6 1.0 dynamic-slice_multiply_fusion
  176.6 0.9 add_bitcast_fusion
  (2 shorter events, 0.0 us)
Async XLA Ops:
  10.9 5.8 %collective-permute-start = (f32[4096,192]{0,1:T(8,128)S(1)}, f32[4096,192]{0,1:T(8,128)S(1)}, u32[]{:S(2)}, u32[]{:S(2)}) collective-permute-start(f32[4096,192]{0,1:T(8,128)S(1)} %convolution_bitcast_fusion), channel_id=1, source_target_pairs={{0,1},{1,0},{2,3},{3,2},{4,5},{5,4},{6,7},{7,6},{8,9},{9,8},{10,11... | collective-permute-start | bytes 9437192 | tf_op jit(solution)/shard_map/ppermute | solution.py:30
  17.1 73.5 %copy-start = (s32[3,16384]{1,0:T(4,128)S(1)}, s32[3,16384]{1,0:T(4,128)}, u32[]{:S(2)}) copy-start(s32[3,16384]{1,0:T(4,128)} %param.3) | copy-start | bytes 589828
  17.1 71.3 %collective-permute-start.1 = (f32[4096,192]{0,1:T(8,128)S(1)}, f32[4096,192]{0,1:T(8,128)S(1)}, u32[]{:S(2)}, u32[]{:S(2)}) collective-permute-start(f32[4096,192]{0,1:T(8,128)S(1)} %add.32), channel_id=1, source_target_pairs={{0,2},{1,3},{2,0},{3,1},{4,6},{5,7},{6,4},{7,5},{8,10},{9,11},{10,... | collective-permute-start | bytes 9437192 | tf_op jit(solution)/shard_map/ppermute | solution.py:30
  88.8 69.7 %collective-permute-start.2 = (f32[4096,192]{0,1:T(8,128)S(1)}, f32[4096,192]{0,1:T(8,128)}, u32[]{:S(2)}, u32[]{:S(2)}) collective-permute-start(f32[4096,192]{0,1:T(8,128)S(1)} %add.33), channel_id=1, source_target_pairs={{0,4},{1,5},{2,6},{3,7},{4,0},{5,1},{6,2},{7,3},{8,12},{9,13},{10,... | collective-permute-start | bytes 9437192 | tf_op jit(solution)/shard_map/ppermute | solution.py:30
